TPU v7x, 512 devices: a whole 4x4x16 slice. The times are simulated.
512 devices in a mesh: dp: 32 (over z, y_hi), expert: 16 (over y_lo, x, core).
Axes of the slice: x: 4, y: 4 (y_hi: 2, y_lo: 2; y = y_hi * 2 + y_lo), z: 16, core: 2. Of those that a mesh axis runs over, the one named last changes fastest.
Arguments:
- weight: bfloat16 [16, 1024, 4096], P('expert', None, 'dp'), may hold values from -0.1875 to 0.1875
- first_moment: float32 [16, 1024, 4096], P('expert', None, 'dp'), may hold values from -3 to 3
- second_moment: float32 [16, 1024, 4096], P('expert', None, 'dp'), may hold values from 0.01 to 1
- gate_act: bfloat16 [16, 4096, 1024], P('expert', 'dp'), may hold values from -6 to 6
- up_act: bfloat16 [16, 4096, 1024], P('expert', 'dp'), may hold values from -6 to 6
- out_grad: bfloat16 [16, 4096, 4096], P('expert', 'dp'), may hold values from -0.29882812 to 0.29882812
- old_host: int32 [16], replicated, may hold values from 0 to 15, each once
- new_host: int32 [16], replicated, may hold values from 0 to 15, each once
- counts: int32 [32, 16], replicated, may hold values from 1 to 128, as said below
Outputs:
- expert_out: bfloat16 [16, 4096, 4096], P('expert', 'dp')
- new_weight: bfloat16 [16, 1024, 4096], P('expert', None, 'dp')
- new_first: float32 [16, 1024, 4096], P('expert', None, 'dp')
- new_second: float32 [16, 1024, 4096], P('expert', None, 'dp')
Inputs may be any that keep to these rules, and one draw needn't show every extreme that they name: `old_host`: each expert's host index appears once. `new_host`: each expert's host index appears once. `counts`: some expert from some replica fills all 128 slots.
All inputs are finite; a program needn't handle non-finite values.
Results may differ from a plain program's by a relative error of at most 0.0049.
Values may be sent and summed in bfloat16 or wider, within the bound.
No kernel may reach another device: no remote copies, remote signals or barrier semaphores. Data moves between devices by JAX's collectives and lax.ppermute only.
A program may use at most 64 MiB of HBM per device.

v0:
```python
import jax
import jax.numpy as jnp
from jax import lax
from jax.sharding import PartitionSpec as P

beta_one = 0.9
beta_two = 0.999
learning_rate = 0.001
epsilon_value = 1e-08
bias_one = 0.9999734386011124
bias_two = 0.0952078528863


def local(
    weight, first_moment, second_moment, gate_act, up_act, out_grad, old_host, new_host, counts
):
    host_count = lax.axis_size("expert")
    my_host = lax.axis_index("expert")
    my_replica = lax.axis_index("dp")
    expert_ids = jnp.arange(new_host.shape[0], dtype=jnp.int32)
    host_ids = jnp.arange(host_count, dtype=jnp.int32)
    matches = new_host[None, :] == host_ids[:, None]
    source_of = jnp.sum(jnp.where(matches, old_host[None, :], 0), axis=1)
    expert_of = jnp.sum(jnp.where(matches, expert_ids[None, :], 0), axis=1)
    my_expert = expert_of[my_host]
    my_source = source_of[my_host]
    hidden_units = weight.shape[1]
    columns = weight.shape[2]
    block_rows = hidden_units // host_count

    def reorder(received):
        return received.reshape(host_count, block_rows, columns)[source_of].reshape(
            hidden_units, columns
        )

    shards = lax.all_gather(weight, "expert", axis=0, tiled=True)
    picked = jnp.arange(shards.shape[0], dtype=jnp.int32) == my_source
    moved_weight = jnp.sum(jnp.where(picked[:, None, None], shards, jnp.zeros_like(shards)), axis=0)
    spread_first, spread_second = (
        lax.all_to_all(first_moment[0], "expert", split_axis=0, concat_axis=0, tiled=True),
        lax.all_to_all(second_moment[0], "expert", split_axis=0, concat_axis=0, tiled=True),
    )
    moved_first, moved_second = (
        lax.all_to_all(reorder(spread_first), "expert", split_axis=0, concat_axis=0, tiled=True),
        lax.all_to_all(reorder(spread_second), "expert", split_axis=0, concat_axis=0, tiled=True),
    )
    live_rows = counts[:, my_expert]
    slot_ids = jnp.arange(gate_act.shape[1], dtype=jnp.int32)
    filled = slot_ids < live_rows[my_replica]
    activated = jax.nn.silu(gate_act[0].astype(jnp.float32)) * up_act[0].astype(jnp.float32)
    hidden = jnp.where(filled[:, None], activated, jnp.float32(0.0)).astype(jnp.bfloat16)
    grad_columns = lax.all_to_all(out_grad[0], "dp", split_axis=1, concat_axis=0, tiled=True)
    shards = lax.all_gather(hidden, "dp", axis=0, tiled=True)
    grad_sum = jnp.einsum("rf,rc->fc", shards, grad_columns, preferred_element_type=jnp.float32)
    produced = jnp.dot(shards, moved_weight, preferred_element_type=jnp.float32).astype(
        jnp.bfloat16
    )
    output_columns = produced
    grad_sum, output_columns = (grad_sum, output_columns)
    output = lax.all_to_all(output_columns, "dp", split_axis=0, concat_axis=1, tiled=True)
    new_first = beta_one * moved_first + (1.0 - beta_one) * grad_sum
    new_second = beta_two * moved_second + (1.0 - beta_two) * grad_sum * grad_sum
    update = (
        learning_rate * (new_first / bias_one) / (jnp.sqrt(new_second / bias_two) + epsilon_value)
    )
    new_weight = (moved_weight.astype(jnp.float32) - update).astype(jnp.bfloat16)
    return (output[None], new_weight[None], new_first[None], new_second[None])


def solution(mesh):
    return jax.shard_map(
        local,
        mesh=mesh,
        in_specs=(
            P("expert", None, "dp"),
            P("expert", None, "dp"),
            P("expert", None, "dp"),
            P("expert", "dp", None),
            P("expert", "dp", None),
            P("expert", "dp", None),
            P(),
            P(),
            P(),
        ),
        out_specs=(
            P("expert", "dp", None),
            P("expert", None, "dp"),
            P("expert", None, "dp"),
            P("expert", None, "dp"),
        ),
        check_vma=False,
    )
```

profile of v0, /device:TPU:2, one launch (start us, length us, event | category | flops | bytes accessed | tf_op | source)
XLA Modules:
  0.0 364.8 jit_solution(6703636606916573695)
XLA Ops:
  7.2 0.0 all-gather.5.cloned.1.call-start
  7.2 0.7 all-gather.5.cloned.1.call-update
  7.9 0.0 all-gather.3.cloned.1.call-start
  7.9 0.8 select_reduce_fusion.1
  8.7 0.6 dynamic_slice.10
  11.3 1.3 dynamic_slice.11
  12.6 0.6 iota_compare_fusion.2
  13.2 1.9 fusion.6
  15.1 0.0 all-gather.3.cloned.1.call-update
  15.2 17.0 %all_to_all.65 = f32[16,64,128]{2,1,0:T(8,128)S(1)} all-to-all(f32[16,64,128]{2,1,0:T(8,128)} %bitcast.38), channel_id=1, replica_groups=mesh['dp'=32,'expert'=16] {'expert'}, dimensions={0} | all-to-all | bytes 1048576 | tf_op jit(solution)/shard_map/all_to_all | solution.py:41
  32.2 6.7 %all-to-all-start.1 = ((f32[16,64,128]{2,1,0:T(8,128)}), f32[16,64,128]{2,1,0:T(8,128)S(1)}, u32[]{:S(2)}, u32[]{:S(2)}) async-start(f32[16,64,128]{2,1,0:T(8,128)} %bitcast.39), calls=%async_computation.1 | async-start | bytes 1048576 | tf_op jit(solution)/shard_map/all_to_all | solution.py:40
  38.9 1.4 gather_fusion.1
  40.2 10.6 %all-to-all-done.1 = f32[16,64,128]{2,1,0:T(8,128)S(1)} async-done(((f32[16,64,128]{2,1,0:T(8,128)}), f32[16,64,128]{2,1,0:T(8,128)S(1)}, u32[]{:S(2)}, u32[]{:S(2)}) %all-to-all-start.1) | async-done | bytes 524320 | tf_op jit(solution)/shard_map/all_to_all | solution.py:40
  50.8 6.4 %all-to-all-start.5 = ((f32[16,64,128]{2,1,0:T(8,128)}), f32[16,64,128]{2,1,0:T(8,128)S(1)}, u32[]{:S(2)}, u32[]{:S(2)}) async-start(f32[16,64,128]{2,1,0:T(8,128)} %gather_fusion.1), calls=%async_computation.5 | async-start | bytes 1048576 | tf_op jit(solution)/shard_map/all_to_all | solution.py:45
  57.2 1.4 gather_fusion
  58.6 7.7 %all-to-all-done.5 = f32[16,64,128]{2,1,0:T(8,128)S(1)} async-done(((f32[16,64,128]{2,1,0:T(8,128)}), f32[16,64,128]{2,1,0:T(8,128)S(1)}, u32[]{:S(2)}, u32[]{:S(2)}) %all-to-all-start.5) | async-done | bytes 524320 | tf_op jit(solution)/shard_map/all_to_all | solution.py:45
  66.3 5.5 %all-to-all-start.2 = ((f32[16,64,128]{2,1,0:T(8,128)}), f32[16,64,128]{2,1,0:T(8,128)S(1)}, u32[]{:S(2)}, u32[]{:S(2)}) async-start(f32[16,64,128]{2,1,0:T(8,128)} %gather_fusion), calls=%async_computation.2 | async-start | bytes 1048576 | tf_op jit(solution)/shard_map/all_to_all | solution.py:44
  71.8 2.3 copy.22
  74.1 5.4 %all-to-all-done.2 = f32[16,64,128]{2,1,0:T(8,128)S(1)} async-done(((f32[16,64,128]{2,1,0:T(8,128)}), f32[16,64,128]{2,1,0:T(8,128)S(1)}, u32[]{:S(2)}, u32[]{:S(2)}) %all-to-all-start.2) | async-done | bytes 524320 | tf_op jit(solution)/shard_map/all_to_all | solution.py:44
  79.5 14.5 %all-to-all-start.3 = ((bf16[128,32,128]{0,2,1:T(8,128)(2,1)}), bf16[128,32,128]{0,2,1:T(8,128)(2,1)S(1)}, u32[]{:S(2)}, u32[]{:S(2)}) async-start(bf16[128,32,128]{0,2,1:T(8,128)(2,1)} %bitcast.12), calls=%async_computation.3 | async-start | bytes 2097152 | tf_op jit(solution)/shard_map/all_to_all | solution.py:52
  94.0 0.6 dynamic_slice.12
  94.6 0.7 iota_compare_fusion.1
  95.2 0.0 all-gather.5.cloned.1.call-done
  95.3 3.1 select_reduce_fusion
  98.4 196.5 %all-gather.3.cloned.1.call-done = bf16[4096,1024]{1,0:T(8,128)(2,1)} async-done(((bf16[128,1024]{1,0:T(8,128)(2,1)}), bf16[4096,1024]{1,0:T(8,128)(2,1)}) %all-gather.3.cloned.1.call-update) | async-done | bytes 8388624 | tf_op jit(solution)/shard_map/all_gather | solution.py:53
  294.9 6.7 %convolution_convert_fusion = bf16[4096,128]{1,0:T(8,128)(2,1)} fusion(bf16[4096,1024]{1,0:T(8,128)(2,1)} %all-gather.3.cloned.1.call-done, bf16[1024,128]{1,0:T(8,128)(2,1)S(1)} %select_reduce_fusion), kind=kOutput, calls=%fused_computation.2 | convolution fusion | flops 1074266112 | bytes 9699328 | tf_op jit(solution)/shard_map/dot_general | solution.py:55
  301.6 0.0 all-to-all-done.3
  301.6 7.6 %all-to-all-start = ((bf16[32,128,128]{2,1,0:T(8,128)(2,1)}), bf16[32,128,128]{2,1,0:T(8,128)(2,1)S(1)}, u32[]{:S(2)}, u32[]{:S(2)}) async-start(bf16[32,128,128]{2,1,0:T(8,128)(2,1)} %bitcast.36), calls=%async_computation | async-start | bytes 2097152 | tf_op jit(solution)/shard_map/all_to_all | solution.py:60
  309.2 0.9 broadcast_multiply_fusion
  310.0 0.9 broadcast_multiply_fusion.1
  310.9 0.7 copy.23
  311.6 7.1 %fusion.7 = (bf16[1,1024,128]{2,1,0:T(8,128)(2,1)}, f32[1024,128]{1,0:T(8,128)}, f32[1024,128]{1,0:T(8,128)}) fusion(bf16[1024,128]{1,0:T(8,128)(2,1)S(1)} %select_reduce_fusion, f32[16,64,128]{2,1,0:T(8,128)} %broadcast_multiply_fusion.1, f32[16,64,128]{2,1,0:T(8,128)} %broadcast_multiply_fusion, bf16[4096,1024]{1,0:T(8,128)(2,1)} %all-gather.3.cloned.1.call-done, ...), kind=kOutput, calls=%fused_computation.18 | convolution fusion | flops 1075314688 | bytes 12058624 | tf_op jit(solution)/shard_map/rf,rc->fc/dot_general | solution.py:54
  318.8 37.2 %all-to-all-done = bf16[32,128,128]{2,1,0:T(8,128)(2,1)S(1)} async-done(((bf16[32,128,128]{2,1,0:T(8,128)(2,1)}), bf16[32,128,128]{2,1,0:T(8,128)(2,1)S(1)}, u32[]{:S(2)}, u32[]{:S(2)}) %all-to-all-start) | async-done | bytes 1048608 | tf_op jit(solution)/shard_map/all_to_all | solution.py:60
  356.0 0.7 copy.21
  356.7 1.3 broadcast_in_dim.68
  (2 shorter events, 0.0 us)
Async XLA Ops:
  7.2 88.1 %all-gather.5.cloned.1.call-start = ((), (), s32[]{:S(2)}) async-start(), calls=%async_computation.7 | async-start | bytes 4456448 | tf_op jit(solution)/shard_map/all_gather | solution.py:36
  7.9 287.0 %all-gather.3.cloned.1.call-start = ((), (), s32[]{:S(2)}) async-start(), calls=%async_computation.6 | async-start | bytes 8650752 | tf_op jit(solution)/shard_map/all_gather | solution.py:53
  32.2 18.6 %all-to-all-start.1 = ((f32[16,64,128]{2,1,0:T(8,128)}), f32[16,64,128]{2,1,0:T(8,128)S(1)}, u32[]{:S(2)}, u32[]{:S(2)}) async-start(f32[16,64,128]{2,1,0:T(8,128)} %bitcast.39), calls=%async_computation.1 | async-start | bytes 1048576 | tf_op jit(solution)/shard_map/all_to_all | solution.py:40
  50.8 15.5 %all-to-all-start.5 = ((f32[16,64,128]{2,1,0:T(8,128)}), f32[16,64,128]{2,1,0:T(8,128)S(1)}, u32[]{:S(2)}, u32[]{:S(2)}) async-start(f32[16,64,128]{2,1,0:T(8,128)} %gather_fusion.1), calls=%async_computation.5 | async-start | bytes 1048576 | tf_op jit(solution)/shard_map/all_to_all | solution.py:45
  66.3 13.2 %all-to-all-start.2 = ((f32[16,64,128]{2,1,0:T(8,128)}), f32[16,64,128]{2,1,0:T(8,128)S(1)}, u32[]{:S(2)}, u32[]{:S(2)}) async-start(f32[16,64,128]{2,1,0:T(8,128)} %gather_fusion), calls=%async_computation.2 | async-start | bytes 1048576 | tf_op jit(solution)/shard_map/all_to_all | solution.py:44
  79.5 222.0 %all-to-all-start.3 = ((bf16[128,32,128]{0,2,1:T(8,128)(2,1)}), bf16[128,32,128]{0,2,1:T(8,128)(2,1)S(1)}, u32[]{:S(2)}, u32[]{:S(2)}) async-start(bf16[128,32,128]{0,2,1:T(8,128)(2,1)} %bitcast.12), calls=%async_computation.3 | async-start | bytes 2097152 | tf_op jit(solution)/shard_map/all_to_all | solution.py:52
  301.6 54.4 %all-to-all-start = ((bf16[32,128,128]{2,1,0:T(8,128)(2,1)}), bf16[32,128,128]{2,1,0:T(8,128)(2,1)S(1)}, u32[]{:S(2)}, u32[]{:S(2)}) async-start(bf16[32,128,128]{2,1,0:T(8,128)(2,1)} %bitcast.36), calls=%async_computation | async-start | bytes 2097152 | tf_op jit(solution)/shard_map/all_to_all | solution.py:60
Sparse Core Ops, SparseCore 0:
  10.1 57.1 all-gather.4
  71.0 223.7 all-gather.2
where the time goes:
time: 366 us; the launch traced here: 365 us
  waiting for transfers between devices  258 us (70%)
  starting transfers between devices  40.7 us (11%)
  blocking collectives  17 us (5%)
  between operations  16.1 us (4%)
  matrix products  13.8 us (4%)
  local copies, waits for them, and re-layouts  10.1 us (3%)
  other arithmetic  8.89 us (2%)
    all_gather x1, waiting for transfers between devices, local(): shards = lax.all_gather(hidden, 'dp', axis=0, tiled=True)  196 us
    all_to_all x1, waiting for transfers between devices, local(): lax.all_to_all(output_columns, 'dp', split_axis=0, concat_axis=1, tiled=T...  37.2 us
    all_to_all x1, blocking collectives, local(): lax.all_to_all(second_moment[0], 'expert', split_axis=0, concat_axis=0, t...  17 us
    all_to_all x1, starting transfers between devices, local(): lax.all_to_all(out_grad[0], 'dp', split_axis=1, concat_axis=0, tiled=True)  14.5 us
    all_to_all x1, waiting for transfers between devices, local(): lax.all_to_all(first_moment[0], 'expert', split_axis=0, concat_axis=0, ti...  10.6 us
    all_to_all x1, waiting for transfers between devices, local(): lax.all_to_all(reorder(spread_second), 'expert', split_axis=0, concat_axi...  7.74 us
    all_to_all x1, starting transfers between devices, local(): lax.all_to_all(output_columns, 'dp', split_axis=0, concat_axis=1, tiled=T...  7.6 us
  transfers between devices with their start and end apart: 7, of which 5 were waited for; matrix products, arithmetic and copies ran while one was open for 8% of the time, Pallas kernels for 0%

commit v1 on v0

--- a/solution.py
+++ b/solution.py
@@ -50,7 +50,9 @@
     activated = jax.nn.silu(gate_act[0].astype(jnp.float32)) * up_act[0].astype(jnp.float32)
     hidden = jnp.where(filled[:, None], activated, jnp.float32(0.0)).astype(jnp.bfloat16)
     grad_columns = lax.all_to_all(out_grad[0], "dp", split_axis=1, concat_axis=0, tiled=True)
-    shards = lax.all_gather(hidden, "dp", axis=0, tiled=True)
+    shards = jnp.concatenate(
+        lax.all_to_all(jnp.stack([hidden] * lax.axis_size("dp")), "dp", 0, 0), axis=0
+    )
     grad_sum = jnp.einsum("rf,rc->fc", shards, grad_columns, preferred_element_type=jnp.float32)
     produced = jnp.dot(shards, moved_weight, preferred_element_type=jnp.float32).astype(
         jnp.bfloat16

time: 366 us -> 590 us (1.61)
  the two profiles are of different devices: /device:TPU:2 before, /device:TPU:56 now
where the time goes in v1:
time: 590 us; the launch traced here: 589 us
  waiting for transfers between devices  461 us (78%)
  starting transfers between devices  50.1 us (8%)
  local copies, waits for them, and re-layouts  26.3 us (4%)
  between operations  16.1 us (3%)
  blocking collectives  15.3 us (3%)
  matrix products  13.6 us (2%)
  other arithmetic  6.51 us (1%)
    all_to_all x1, waiting for transfers between devices, local(): lax.all_to_all(jnp.stack([hidden] * lax.axis_size('dp')), 'dp', 0, 0)  363 us
    all_to_all x1, waiting for transfers between devices, local(): lax.all_to_all(output_columns, 'dp', split_axis=0, concat_axis=1, tiled=T...  47.2 us
    all_to_all x1, waiting for transfers between devices, local(): lax.all_to_all(out_grad[0], 'dp', split_axis=1, concat_axis=0, tiled=True)  31.4 us
    all_to_all x1, starting transfers between devices, local(): lax.all_to_all(jnp.stack([hidden] * lax.axis_size('dp')), 'dp', 0, 0)  17.9 us
    all_to_all x1, blocking collectives, local(): lax.all_to_all(second_moment[0], 'expert', split_axis=0, concat_axis=0, t...  15.3 us
    all_to_all x1, local copies, waits for them, and re-layouts, local(): lax.all_to_all(jnp.stack([hidden] * lax.axis_size('dp')), 'dp', 0, 0)  11.9 us
  transfers between devices with their start and end apart: 7, of which 6 were waited for; matrix products, arithmetic and copies ran while one was open for 7% of the time, Pallas kernels for 0%

profile of v1, /device:TPU:56, one launch (start us, length us, event | category | flops | bytes accessed | tf_op | source)
XLA Modules:
  0.0 589.0 jit_solution(15483867930072437571)
XLA Ops:
  7.2 15.3 %all_to_all.67 = f32[16,64,128]{2,1,0:T(8,128)S(1)} all-to-all(f32[16,64,128]{2,1,0:T(8,128)} %bitcast.41), channel_id=1, replica_groups=mesh['dp'=32,'expert'=16] {'expert'}, dimensions={0} | all-to-all | bytes 1048576 | tf_op jit(solution)/shard_map/all_to_all | solution.py:41
  22.4 4.9 all-to-all-start.2
  27.3 0.8 select_reduce_fusion.1
  28.1 1.4 gather_fusion.1
  29.5 7.3 %all-to-all-done.2 = f32[16,64,128]{2,1,0:T(8,128)S(1)} async-done(((f32[16,64,128]{2,1,0:T(8,128)}), f32[16,64,128]{2,1,0:T(8,128)S(1)}, u32[]{:S(2)}, u32[]{:S(2)}) %all-to-all-start.2) | async-done | bytes 524320 | tf_op jit(solution)/shard_map/all_to_all | solution.py:40
  36.8 4.9 all-to-all-start.6
  41.7 1.4 gather_fusion
  43.1 8.1 %all-to-all-done.6 = f32[16,64,128]{2,1,0:T(8,128)S(1)} async-done(((f32[16,64,128]{2,1,0:T(8,128)}), f32[16,64,128]{2,1,0:T(8,128)S(1)}, u32[]{:S(2)}, u32[]{:S(2)}) %all-to-all-start.6) | async-done | bytes 524320 | tf_op jit(solution)/shard_map/all_to_all | solution.py:45
  51.2 4.9 all-to-all-start.3
  56.1 0.6 dynamic_slice.10
  58.7 1.3 dynamic_slice.11
  59.9 0.6 iota_compare_fusion.2
  60.6 1.2 fusion.8
  61.8 0.2 copy.25
  62.0 3.6 all-to-all-done.3
  65.6 5.1 stack.5
  70.7 0.0 copy-start
  70.7 17.9 %all-to-all-start = ((bf16[32,128,1024]{1,2,0:T(8,128)(2,1)}), bf16[32,128,1024]{1,2,0:T(8,128)(2,1)}, u32[]{:S(2)}, u32[]{:S(2)}) async-start(bf16[32,128,1024]{1,2,0:T(8,128)(2,1)} %stack.5), calls=%async_computation | async-start | bytes 16777216 | tf_op jit(solution)/shard_map/all_to_all | solution.py:54
  88.7 0.0 all-gather.2.cloned.1.call-start
  88.7 0.7 all-gather.2.cloned.1.call-update
  89.4 0.0 copy-done
  89.4 0.7 copy.28
  90.1 1.3 copy.29
  91.4 362.7 %all-to-all-done = bf16[32,128,1024]{1,2,0:T(8,128)(2,1)} async-done(((bf16[32,128,1024]{1,2,0:T(8,128)(2,1)}), bf16[32,128,1024]{1,2,0:T(8,128)(2,1)}, u32[]{:S(2)}, u32[]{:S(2)}) %all-to-all-start) | async-done | bytes 8388640 | tf_op jit(solution)/shard_map/all_to_all | solution.py:54
  454.1 11.3 %all-to-all-start.4 = ((bf16[128,32,128]{2,0,1:T(8,128)(2,1)}), bf16[128,32,128]{2,0,1:T(8,128)(2,1)S(1)}, u32[]{:S(2)}, u32[]{:S(2)}) async-start(bf16[128,32,128]{2,0,1:T(8,128)(2,1)} %copy.29), calls=%async_computation.4 | async-start | bytes 2097152 | tf_op jit(solution)/shard_map/all_to_all | solution.py:52
  465.4 0.6 dynamic_slice.12
  466.0 0.6 iota_compare_fusion.1
  466.7 0.0 all-gather.2.cloned.1.call-done
  466.7 3.1 select_reduce_fusion
  469.8 11.9 %copy.26 = bf16[32,128,1024]{2,1,0:T(8,128)(2,1)} copy(bf16[32,128,1024]{1,2,0:T(8,128)(2,1)} %all-to-all-done) | data formatting | bytes 16777216 | tf_op jit(solution)/shard_map/all_to_all | solution.py:54
  481.7 6.7 %convolution_convert_fusion = bf16[4096,128]{1,0:T(8,128)(2,1)} fusion(bf16[4096,1024]{1,0:T(8,128)(2,1)} %bitcast.37, bf16[1024,128]{1,0:T(8,128)(2,1)S(1)} %select_reduce_fusion), kind=kOutput, calls=%fused_computation.2 | convolution fusion | flops 1074266112 | bytes 9699328 | tf_op jit(solution)/shard_map/dot_general | solution.py:57
  488.4 31.4 %all-to-all-done.4 = bf16[128,32,128]{2,0,1:T(8,128)(2,1)S(1)} async-done(((bf16[128,32,128]{2,0,1:T(8,128)(2,1)}), bf16[128,32,128]{2,0,1:T(8,128)(2,1)S(1)}, u32[]{:S(2)}, u32[]{:S(2)}) %all-to-all-start.4) | async-done | bytes 1048608 | tf_op jit(solution)/shard_map/all_to_all | solution.py:52
  519.8 6.1 %all-to-all-start.1 = ((bf16[32,128,128]{2,1,0:T(8,128)(2,1)}), bf16[32,128,128]{2,1,0:T(8,128)(2,1)S(1)}, u32[]{:S(2)}, u32[]{:S(2)}) async-start(bf16[32,128,128]{2,1,0:T(8,128)(2,1)} %bitcast.40), calls=%async_computation.1 | async-start | bytes 2097152 | tf_op jit(solution)/shard_map/all_to_all | solution.py:62
  526.0 0.1 broadcast_multiply_fusion
  526.0 0.1 broadcast_multiply_fusion.1
  526.1 6.9 %fusion.9 = (bf16[1,1024,128]{2,1,0:T(8,128)(2,1)}, f32[1024,128]{1,0:T(8,128)}, f32[1024,128]{1,0:T(8,128)}) fusion(bf16[1024,128]{1,0:T(8,128)(2,1)S(1)} %select_reduce_fusion, f32[16,64,128]{2,1,0:T(8,128)S(1)} %broadcast_multiply_fusion.1, f32[16,64,128]{2,1,0:T(8,128)S(1)} %broadcast_multiply_fusion, bf16[32,128,1024]{1,2,0:T(8,128)(2,1)} %all-to-all-done, ...), kind=kOutput, calls=%fused_computation.21 | convolution fusion | flops 1075314688 | bytes 12058624 | tf_op jit(solution)/shard_map/rf,rc->fc/dot_general | solution.py:56
  533.0 47.2 %all-to-all-done.1 = bf16[32,128,128]{2,1,0:T(8,128)(2,1)S(1)} async-done(((bf16[32,128,128]{2,1,0:T(8,128)(2,1)}), bf16[32,128,128]{2,1,0:T(8,128)(2,1)S(1)}, u32[]{:S(2)}, u32[]{:S(2)}) %all-to-all-start.1) | async-done | bytes 1048608 | tf_op jit(solution)/shard_map/all_to_all | solution.py:62
  580.2 0.7 copy.27
  580.9 1.3 broadcast_in_dim.68
  (2 shorter events, 0.0 us)
Async XLA Ops:
  22.4 14.4 %all-to-all-start.2 = ((f32[16,64,128]{2,1,0:T(8,128)}), f32[16,64,128]{2,1,0:T(8,128)S(1)}, u32[]{:S(2)}, u32[]{:S(2)}) async-start(f32[16,64,128]{2,1,0:T(8,128)} %bitcast.42), calls=%async_computation.2 | async-start | bytes 1048576 | tf_op jit(solution)/shard_map/all_to_all | solution.py:40
  36.8 14.4 %all-to-all-start.6 = ((f32[16,64,128]{2,1,0:T(8,128)}), f32[16,64,128]{2,1,0:T(8,128)S(1)}, u32[]{:S(2)}, u32[]{:S(2)}) async-start(f32[16,64,128]{2,1,0:T(8,128)} %gather_fusion.1), calls=%async_computation.6 | async-start | bytes 1048576 | tf_op jit(solution)/shard_map/all_to_all | solution.py:45
  51.2 14.4 %all-to-all-start.3 = ((f32[16,64,128]{2,1,0:T(8,128)}), f32[16,64,128]{2,1,0:T(8,128)S(1)}, u32[]{:S(2)}, u32[]{:S(2)}) async-start(f32[16,64,128]{2,1,0:T(8,128)} %gather_fusion), calls=%async_computation.3 | async-start | bytes 1048576 | tf_op jit(solution)/shard_map/all_to_all | solution.py:44
  70.7 18.7 %copy-start = (bf16[1,128,4096]{2,1,0:T(8,128)(2,1)S(1)}, bf16[1,128,4096]{2,1,0:T(8,128)(2,1)}, u32[]{:S(2)}) copy-start(bf16[1,128,4096]{2,1,0:T(8,128)(2,1)} %param.14) | copy-start | bytes 3145732
  70.7 383.4 %all-to-all-start = ((bf16[32,128,1024]{1,2,0:T(8,128)(2,1)}), bf16[32,128,1024]{1,2,0:T(8,128)(2,1)}, u32[]{:S(2)}, u32[]{:S(2)}) async-start(bf16[32,128,1024]{1,2,0:T(8,128)(2,1)} %stack.5), calls=%async_computation | async-start | bytes 16777216 | tf_op jit(solution)/shard_map/all_to_all | solution.py:54
  88.7 378.0 %all-gather.2.cloned.1.call-start = ((), (), s32[]{:S(2)}) async-start(), calls=%async_computation.7 | async-start | bytes 4456448 | tf_op jit(solution)/shard_map/all_gather | solution.py:36
  454.1 65.7 %all-to-all-start.4 = ((bf16[128,32,128]{2,0,1:T(8,128)(2,1)}), bf16[128,32,128]{2,0,1:T(8,128)(2,1)S(1)}, u32[]{:S(2)}, u32[]{:S(2)}) async-start(bf16[128,32,128]{2,0,1:T(8,128)(2,1)} %copy.29), calls=%async_computation.4 | async-start | bytes 2097152 | tf_op jit(solution)/shard_map/all_to_all | solution.py:52
  519.8 60.4 %all-to-all-start.1 = ((bf16[32,128,128]{2,1,0:T(8,128)(2,1)}), bf16[32,128,128]{2,1,0:T(8,128)(2,1)S(1)}, u32[]{:S(2)}, u32[]{:S(2)}) async-start(bf16[32,128,128]{2,1,0:T(8,128)(2,1)} %bitcast.40), calls=%async_computation.1 | async-start | bytes 2097152 | tf_op jit(solution)/shard_map/all_to_all | solution.py:62
Sparse Core Ops, SparseCore 0:
  91.7 45.7 all-gather.1
